TPU v7x, 32 devices: a whole 2x2x4 slice. The times are simulated.
32 devices in a mesh: pairs: 2 (over y), pb: 4 (over z), ka: 2 (over core), wa: 2 (over x).
Axes of the slice: x: 2, y: 2, z: 4, core: 2. Of those that a mesh axis runs over, the one named last changes fastest.
Arguments:
- clean_rows: bfloat16 [4096, 8192], P(('pairs', 'pb', 'ka'), 'wa'), parts along dimension 0, may hold values from -72 to 72
- noised_rows: bfloat16 [4096, 8192], P(('pairs', 'pb', 'ka'), 'wa'), parts along dimension 0, may hold values from -6 to 6
- query_weight: bfloat16 [8192, 512], P('wa'), may hold values from -0.0625 to 0.0625
- key_weight: bfloat16 [8192, 128], P('wa'), may hold values from -0.0625 to 0.0625
- value_weight: bfloat16 [8192, 128], P('wa'), may hold values from -0.0625 to 0.0625
- out_grads: bfloat16 [4096, 512], P(('pairs', 'pb', 'ka'), 'wa'), parts along dimension 0, may hold values from -6 to 6
- lookback: int32 [4096], P('pairs'), parts along dimension 0, may hold values from 1 to 2048
Outputs:
- attribution: float32 [4096], P(('pairs', 'pb', 'ka', 'wa')), parts along dimension 0
There are 2 independent parts, one for each index of `pairs`. A program takes and returns all parts, laid end to end along the dimension named above; an argument that names none is the same for every part. Nothing has to cross between parts.
All inputs are finite; a program needn't handle non-finite values.
Results may differ from a plain program's by a relative error of at most 0.01315.
The roundings to bfloat16 on the way count: a program that leaves them out, or rounds other values in their place, can miss the bound.
Values may be sent and summed in bfloat16 or wider, within the bound.
No kernel may reach another device: no remote copies, remote signals or barrier semaphores. Data moves between devices by JAX's collectives and lax.ppermute only.
A program may use at most 64 MiB of HBM per device.

v0:
```python
import math
import jax
import jax.numpy as jnp
from jax import lax
from jax.sharding import PartitionSpec as P

very_low = -1e30


def joined(array, axis, combine):
    everything = jax.tree.map(lambda part: lax.all_gather(part, axis), array)
    first = jax.tree.map(lambda part: part[0], everything)

    def turn(k, so_far):
        return combine(so_far, jax.tree.map(lambda part: part[k], everything))

    return lax.fori_loop(1, lax.axis_size(axis), turn, first)


def split_heads(pair_block, head_size):
    return pair_block.reshape(pair_block.shape[0], pair_block.shape[1] // head_size, head_size)


def visible_pairs(query_pos, query_look, key_pos):
    distance = query_pos[:, None] - key_pos[None, :]
    return (distance >= 0) & (distance < query_look[:, None])


def combine_stats(earlier, later):
    highest = jnp.maximum(earlier[0], later[0])
    left_scale = jnp.exp(earlier[0] - highest)
    right_scale = jnp.exp(later[0] - highest)
    return (
        highest,
        earlier[1] * left_scale + later[1] * right_scale,
        earlier[2] * left_scale + later[2] * right_scale,
    )


def block_stats(
    query_block, grad_block, query_pos, query_look, key_block, value_block, key_pos, score_scale
):
    scores = (
        jnp.einsum("bhd,kd->bhk", query_block, key_block, preferred_element_type=jnp.float32)
        * score_scale
    )
    grad_value = jnp.einsum(
        "bhd,kd->bhk", grad_block, value_block, preferred_element_type=jnp.float32
    )
    visible = visible_pairs(query_pos, query_look, key_pos)[:, None, :]
    masked = jnp.where(visible, scores, very_low)
    highest = jnp.max(masked, axis=2)
    weights = jnp.where(visible, jnp.exp(masked - highest[:, :, None]), 0.0)
    return (highest, jnp.sum(weights, axis=2), jnp.sum(weights * grad_value, axis=2))


def block_changes(
    query_block,
    grad_block,
    query_pos,
    query_look,
    row_parts,
    key_block,
    value_block,
    noised_block,
    key_pos,
    score_scale,
):
    highest, row_total, weighted, mean_now = row_parts
    scores = (
        jnp.einsum("bhd,kd->bhk", query_block, key_block, preferred_element_type=jnp.float32)
        * score_scale
    )
    patched = (
        jnp.einsum("bhd,kd->bhk", query_block, noised_block, preferred_element_type=jnp.float32)
        * score_scale
    )
    grad_value = jnp.einsum(
        "bhd,kd->bhk", grad_block, value_block, preferred_element_type=jnp.float32
    )
    visible = visible_pairs(query_pos, query_look, key_pos)[:, None, :]
    held = highest[:, :, None]
    scores = jnp.where(visible, scores, held)
    patched = jnp.where(visible, patched, held)
    shifted = jnp.maximum(held, patched)
    factor = jnp.exp(held - shifted)
    swapped = jnp.exp(patched - shifted) - jnp.exp(scores - shifted)
    divisor = jnp.maximum(row_total[:, :, None] * factor + swapped, 1.0)
    change = (weighted[:, :, None] * factor + swapped * grad_value) / divisor - mean_now[:, :, None]
    return jnp.sum(jnp.where(visible, change, 0.0), axis=(0, 1))


def tile_stats(pair_piece, query_pos, query_look, key_tile, key_pos, score_scale, head_size):
    row_count = pair_piece.shape[0]
    head_cols = pair_piece.shape[1] // 2
    block_rows = math.gcd(row_count, 512)
    key_count = key_tile.shape[0]
    key_width = math.gcd(key_count, 1024)

    def one_block(block_index):
        offset = block_index * block_rows
        pair_block = lax.dynamic_slice_in_dim(pair_piece, offset, block_rows, 0)
        query_block = split_heads(pair_block[:, :head_cols], head_size)
        grad_block = split_heads(pair_block[:, head_cols:], head_size)
        block_pos = lax.dynamic_slice_in_dim(query_pos, offset, block_rows, 0)
        block_look = lax.dynamic_slice_in_dim(query_look, offset, block_rows, 0)
        head_count = query_block.shape[1]

        def one_key(running, key_index):
            key_offset = key_index * key_width
            key_block = lax.dynamic_slice(key_tile, (key_offset, 0), (key_width, head_size))
            value_block = lax.dynamic_slice(
                key_tile, (key_offset, head_size), (key_width, head_size)
            )
            block_keys = lax.dynamic_slice_in_dim(key_pos, key_offset, key_width, 0)
            block_part = block_stats(
                query_block,
                grad_block,
                block_pos,
                block_look,
                key_block,
                value_block,
                block_keys,
                score_scale,
            )
            return (combine_stats(running, block_part), None)

        empty_rows = jnp.zeros((block_rows, head_count), jnp.float32)
        start_stats = (
            jnp.full((block_rows, head_count), very_low, jnp.float32),
            empty_rows,
            empty_rows,
        )
        result, _ = lax.scan(
            one_key, start_stats, jnp.arange(key_count // key_width, dtype=jnp.int32)
        )
        return result

    if block_rows == row_count:
        return one_block(0)
    stacked = lax.map(one_block, jnp.arange(row_count // block_rows, dtype=jnp.int32))
    return tuple((member.reshape(row_count, member.shape[2]) for member in stacked))


def tile_changes(
    pair_tile, query_pos, query_look, merged_stats, key_tile, key_pos, score_scale, head_size
):
    row_count = pair_tile.shape[0]
    head_cols = pair_tile.shape[1] // 2
    block_rows = math.gcd(row_count, 512)
    key_count = key_tile.shape[0]
    key_width = math.gcd(key_count, 1024)
    highest, row_total, weighted = merged_stats
    row_parts = (highest, row_total, weighted, weighted / row_total)

    def one_block(running, block_index):
        offset = block_index * block_rows
        pair_block = lax.dynamic_slice_in_dim(pair_tile, offset, block_rows, 0)
        query_block = split_heads(pair_block[:, :head_cols], head_size)
        grad_block = split_heads(pair_block[:, head_cols:], head_size)
        block_pos = lax.dynamic_slice_in_dim(query_pos, offset, block_rows, 0)
        block_look = lax.dynamic_slice_in_dim(query_look, offset, block_rows, 0)
        block_rows_stats = tuple(
            (lax.dynamic_slice_in_dim(member, offset, block_rows, 0) for member in row_parts)
        )

        def one_key(key_index):
            key_offset = key_index * key_width
            key_block = lax.dynamic_slice(key_tile, (key_offset, 0), (key_width, head_size))
            value_block = lax.dynamic_slice(
                key_tile, (key_offset, head_size), (key_width, head_size)
            )
            noised_block = lax.dynamic_slice(
                key_tile, (key_offset, 2 * head_size), (key_width, head_size)
            )
            block_keys = lax.dynamic_slice_in_dim(key_pos, key_offset, key_width, 0)
            return block_changes(
                query_block,
                grad_block,
                block_pos,
                block_look,
                block_rows_stats,
                key_block,
                value_block,
                noised_block,
                block_keys,
                score_scale,
            )

        changes = lax.map(one_key, jnp.arange(key_count // key_width, dtype=jnp.int32))
        return (running + changes.reshape(key_count), None)

    summed, _ = lax.scan(
        one_block,
        jnp.zeros((key_count,), jnp.float32),
        jnp.arange(row_count // block_rows, dtype=jnp.int32),
    )
    return summed


def shards(clean_rows, noised_rows, query_weight, key_weight, value_weight, out_grads, lookback):
    head_size = key_weight.shape[1]
    score_scale = 1.0 / math.sqrt(head_size)
    pb_size = lax.axis_size("pb")
    ka_size = lax.axis_size("ka")
    pb_index = lax.axis_index("pb")
    ka_index = lax.axis_index("ka")
    pair_rows = clean_rows.shape[0]
    side_weight = jnp.concatenate([key_weight, value_weight], axis=1)
    query_terms = jnp.dot(clean_rows, query_weight, preferred_element_type=jnp.float32)
    queries = lax.psum_scatter(query_terms, "wa", scatter_dimension=1, tiled=True).astype(
        jnp.bfloat16
    )
    key_side = lax.psum_scatter(
        jnp.concatenate(
            [
                jnp.dot(clean_rows, side_weight, preferred_element_type=jnp.float32),
                jnp.dot(noised_rows, key_weight, preferred_element_type=jnp.float32),
            ],
            axis=1,
        ),
        "wa",
        scatter_dimension=0,
        tiled=True,
    ).astype(jnp.bfloat16)
    pair_data = jnp.concatenate([queries, out_grads], axis=1)
    look_grid = lookback.reshape(pb_size, ka_size, pair_rows)
    tile_base = pb_index * (ka_size * pair_rows)
    key_tile = lax.all_gather(key_side, ("pb", "wa"), axis=0, tiled=True)
    row_ids = jnp.arange(key_tile.shape[0], dtype=jnp.int32)
    key_pos = (
        row_ids // pair_rows * (ka_size * pair_rows) + ka_index * pair_rows + row_ids % pair_rows
    )
    look_tile = lax.dynamic_index_in_dim(look_grid, pb_index, 0, keepdims=False).reshape(-1)
    pair_piece = lax.all_gather(pair_data, "ka", axis=0, tiled=True)
    row_ids = jnp.arange(pair_piece.shape[0], dtype=jnp.int32)
    highest, row_total, weighted, pair_tile = tile_stats(
        pair_piece, tile_base + row_ids, look_tile, key_tile, key_pos, score_scale, head_size
    ) + (pair_piece,)
    merged_stats = joined((highest, row_total, weighted), "ka", combine_stats)
    query_pos = tile_base + jnp.arange(pair_tile.shape[0], dtype=jnp.int32)
    key_part = tile_changes(
        pair_tile, query_pos, look_tile, merged_stats, key_tile, key_pos, score_scale, head_size
    )
    return lax.psum_scatter(key_part, ("pb", "wa"), scatter_dimension=0, tiled=True)


def solution(mesh):
    in_specs = (
        P(("pairs", "pb", "ka"), "wa"),
        P(("pairs", "pb", "ka"), "wa"),
        P("wa", None),
        P("wa", None),
        P("wa", None),
        P(("pairs", "pb", "ka"), "wa"),
        P("pairs"),
    )
    out_specs = P(("pairs", "pb", "ka", "wa"))
    return jax.shard_map(shards, mesh=mesh, in_specs=in_specs, out_specs=out_specs, check_vma=False)
```

profile of v0, /device:TPU:0, one launch (start us, length us, event | category | flops | bytes accessed | tf_op | source)
XLA Modules:
  0.0 103.1 jit_solution(1232725400893335930)
XLA Ops:
  6.5 0.0 copy-start
  6.5 0.0 reduce-scatter.5.cloned.1.call-start
  6.5 2.8 %fusion.47 = f32[256,128]{0,1:T(8,128)S(1)} fusion(bf16[256,4096]{1,0:T(8,128)(2,1)} %param.8, bf16[4096,128]{1,0:T(8,128)(2,1)} %param.10), kind=kOutput, calls=%fused_computation.77 | convolution fusion | flops 268435456 | bytes 3276800 | tf_op jit(solution)/shard_map/dot_general | solution.py:218
  9.4 0.0 copy-done
  9.4 2.3 %fusion.10 = f32[256,256]{0,1:T(8,128)S(1)} fusion(bf16[256,4096]{1,0:T(8,128)(2,1)S(1)} %copy-done, bf16[4096,128]{1,0:T(8,128)(2,1)} %param.11, bf16[4096,128]{1,0:T(8,128)(2,1)} %param.10), kind=kOutput, calls=%fused_computation.19 | convolution fusion | flops 541065216 | bytes 4456448 | tf_op jit(solution)/shard_map/dot_general | solution.py:217
  11.7 0.8 pad_maximum_fusion
  12.5 0.0 reduce-scatter.5.cloned.1.call-update
  12.5 0.0 copy-start.2
  12.5 0.0 copy-start.3
  12.5 0.0 copy-start.1
  12.5 0.0 reduce-scatter.3.cloned.1.call-start
  12.6 4.3 %fusion.46 = f32[256,512]{1,0:T(8,128)} fusion(bf16[256,4096]{1,0:T(8,128)(2,1)S(1)} %copy-done, bf16[4096,512]{1,0:T(8,128)(2,1)} %param.9), kind=kOutput, calls=%fused_computation.76 | convolution fusion | flops 1073741824 | bytes 6815744 | tf_op jit(solution)/shard_map/dot_general | solution.py:210
  16.8 0.0 reduce-scatter.3.cloned.1.call-update
  16.9 0.0 copy-done.2
  16.9 0.0 copy-done.3
  17.0 0.6 dynamic-slice
  18.2 0.6 fusion.9
  18.8 9.7 %reduce-scatter.5.cloned.1.call-done = f32[128,384]{0,1:T(8,128)} async-done(((f32[256,384]{0,1:T(8,128)}), f32[128,384]{0,1:T(8,128)}) %reduce-scatter.5.cloned.1.call-update) | async-done | bytes 196624 | tf_op jit(solution)/shard_map/reduce_scatter | solution.py:214
  28.6 0.9 convert_element_type.7
  29.5 32.1 %all_gather.19 = bf16[1024,384]{0,1:T(8,128)(2,1)S(1)} all-gather(bf16[128,384]{0,1:T(8,128)(2,1)S(1)} %convert_element_type.7), channel_id=1, replica_groups=mesh['pairs'=2,'pb'=4,'ka'=2,'wa'=2] {'pb','wa'}, dimensions={0}, use_global_device_ids=true | all-gather | bytes 884736 | tf_op jit(solution)/shard_map/all_gather | solution.py:229
  61.6 0.0 reduce-scatter.3.cloned.1.call-done
  61.6 1.0 convert_element_type.6
  62.6 0.0 copy-done.1
  62.6 2.2 %all_gather.18 = bf16[512,512]{1,0:T(8,128)(2,1)S(1)} all-gather(bf16[256,512]{1,0:T(8,128)(2,1)S(1)} %pad_maximum_fusion.1), channel_id=1, replica_groups=mesh['pairs'=2,'pb'=4,'ka'=2,'wa'=2] {'ka'}, dimensions={0}, use_global_device_ids=true | all-gather | bytes 786432 | tf_op jit(solution)/shard_map/all_gather | solution.py:235
  64.8 1.1 %select_reduce_fusion.1 = (f32[512,2]{0,1:T(2,128)S(1)}, f32[512,2,1024]{2,0,1:T(8,128)S(1)}) fusion(pred[512,1024]{1,0:T(8,128)(4,1)S(1)} %fusion.9, bf16[1024,384]{0,1:T(8,128)(2,1)S(1)} %all_gather.19, bf16[64,2,8,128]{3,2,1,0:T(8,128)(2,1)S(1)} %get-tuple-element.110), kind=kOutput, calls=%fused_computation.10 | convolution fusion | flops 271580160 | bytes 5246976 | tf_op jit(solution)/shard_map/while/body/eval_jaxpr/bhd,kd->bhk/dot_general | solution.py:44
  65.9 2.0 %fusion.4 = (f32[512,2]{0,1:T(2,128)S(1)}, f32[512,2]{0,1:T(2,128)S(1)}, f32[512,2,1024]{2,0,1:T(8,128)S(1)}) fusion(f32[512,2,1024]{2,0,1:T(8,128)S(1)} %get-tuple-element.116, f32[512,2]{0,1:T(2,128)S(1)} %get-tuple-element.115, pred[512,1024]{1,0:T(8,128)(4,1)S(1)} %fusion.9, bf16[1024,384]{0,1:T(8,128)(2,1)S(1)} %all_gather.19, ...), kind=kOutput, calls=%fused_computation.13 | convolution fusion | flops 275773440 | bytes 9449472 | tf_op jit(solution)/shard_map/while/body/eval_jaxpr/bhd,kd->bhk/dot_general | solution.py:47
  67.9 1.8 %all_gather.20 = f32[2,512,2]{1,2,0:T(2,128)S(1)} all-gather(f32[1,512,2]{1,2,0:T(2,128)S(1)} %get-tuple-element.112), channel_id=1, replica_groups=mesh['pairs'=2,'pb'=4,'ka'=2,'wa'=2] {'ka'}, dimensions={0}, use_global_device_ids=true | all-gather | bytes 12288 | tf_op jit(solution)/shard_map/all_gather | solution.py:11
  69.7 1.8 %all_gather.21 = f32[2,512,2]{1,2,0:T(2,128)S(1)} all-gather(f32[1,512,2]{1,2,0:T(2,128)S(1)} %get-tuple-element.114), channel_id=1, replica_groups=mesh['pairs'=2,'pb'=4,'ka'=2,'wa'=2] {'ka'}, dimensions={0}, use_global_device_ids=true | all-gather | bytes 12288 | tf_op jit(solution)/shard_map/all_gather | solution.py:11
  71.5 1.8 %all_gather.22 = f32[2,512,2]{1,2,0:T(2,128)S(1)} all-gather(f32[1,512,2]{1,2,0:T(2,128)S(1)} %get-tuple-element.113), channel_id=1, replica_groups=mesh['pairs'=2,'pb'=4,'ka'=2,'wa'=2] {'ka'}, dimensions={0}, use_global_device_ids=true | all-gather | bytes 12288 | tf_op jit(solution)/shard_map/all_gather | solution.py:11
  73.4 4.5 %select_reduce_fusion = f32[1024]{0:T(1024)S(1)} fusion(f32[512,2,1024]{2,0,1:T(8,128)S(1)} %get-tuple-element.117, f32[512,2,1024]{2,0,1:T(8,128)S(1)} %get-tuple-element.116, f32[512,2]{0,1:T(2,128)S(1)} %get-tuple-element.94, f32[512,2]{0,1:T(2,128)S(1)} %get-tuple-element.107, f32[512,2]{0,1:T(2,128)S(1)} %get-tuple-element.109, ...), kind=kOutput, calls=%fused_computation.7 | convolution fusion | flops 288357376 | bytes 9457664 | tf_op jit(solution)/shard_map/while/body/eval_jaxpr/while/body/eval_jaxpr/bhd,kd->bhk/dot_general | solution.py:75
  77.9 17.8 %all-reduce = f32[1024]{0:T(1024)S(1)} all-reduce(f32[1024]{0:T(1024)S(1)} %select_reduce_fusion), channel_id=4, replica_groups=mesh['pairs'=2,'pb'=4,'ka'=2,'wa'=2] {'pb','wa'}, use_global_device_ids=true, to_apply=%region_6.7.clone | all-reduce | flops 1024 | bytes 8192
  95.7 0.6 dynamic-slice.1
  (9 shorter events, 0.1 us)
Async XLA Ops:
  6.5 2.8 %copy-start = (bf16[256,4096]{1,0:T(8,128)(2,1)S(1)}, bf16[256,4096]{1,0:T(8,128)(2,1)}, u32[]{:S(2)}) copy-start(bf16[256,4096]{1,0:T(8,128)(2,1)} %param.7) | copy-start | bytes 6291460
  6.5 22.0 %reduce-scatter.5.cloned.1.call-start = ((), (), s32[]{:S(2)}) async-start(), calls=%async_computation.3 | async-start | bytes 589824 | tf_op jit(solution)/shard_map/reduce_scatter | solution.py:214
  12.5 4.4 %copy-start.2 = (s32[2048]{0:T(1024)S(1)}, s32[2048]{0:T(1024)}, u32[]{:S(2)}) copy-start(s32[2048]{0:T(1024)} %param.13) | copy-start | bytes 24580
  12.5 4.4 %copy-start.3 = (u32[32]{0:T(128)S(1)}, u32[32]{0:T(128)}, u32[]{:S(2)}) copy-start(u32[32]{0:T(128)} %constant.133) | copy-start | bytes 388
  12.5 50.0 %copy-start.1 = (bf16[256,256]{1,0:T(8,128)(2,1)S(1)}, bf16[256,256]{1,0:T(8,128)(2,1)}, u32[]{:S(2)}) copy-start(bf16[256,256]{1,0:T(8,128)(2,1)} %param.12) | copy-start | bytes 393220
  12.5 49.1 %reduce-scatter.3.cloned.1.call-start = ((), (), s32[]{:S(2)}) async-start(), calls=%async_computation.2 | async-start | bytes 786432 | tf_op jit(solution)/shard_map/reduce_scatter | solution.py:211
Sparse Core Ops, SparseCore 0:
  12.6 15.8 reduce-scatter.4
  30.8 22.4 reduce-scatter.2
where the time goes:
time: 103 us
  blocking collectives  57.5 us (56%)
  matrix products  17 us (17%)
  between operations  14.2 us (14%)
  waiting for transfers between devices  9.76 us (9%)
  other arithmetic  3.36 us (3%)
  local copies, waits for them, and re-layouts  1.25 us (1%)
    all_gather x1, blocking collectives, shards(): key_tile = lax.all_gather(key_side, ('pb', 'wa'), axis=0, tiled=True)  32.1 us
    unnamed x1, blocking collectives  17.8 us
    reduce_scatter x1, waiting for transfers between devices, shards(): lax.psum_scatter(jnp.concatenate([jnp.dot(clean_rows, side_weight, prefer...  9.73 us
    all_gather x3, blocking collectives, joined(): everything = jax.tree.map(lambda part: lax.all_gather(part, axis), array)  5.44 us
    dot_general x1, matrix products, block_changes(): jnp.einsum('bhd,kd->bhk', query_block, noised_block, preferred_element_ty...  4.54 us
    dot_general x1, matrix products, shards(): jnp.dot(clean_rows, query_weight, preferred_element_type=jnp.float32)  4.25 us
    dot_general x1, matrix products, shards(): jnp.dot(noised_rows, key_weight, preferred_element_type=jnp.float32)  2.83 us
    dot_general x1, matrix products, shards(): jnp.dot(clean_rows, side_weight, preferred_element_type=jnp.float32)  2.3 us
  transfers between devices with their start and end apart: 2, of which 1 were waited for; matrix products, arithmetic and copies ran while one was open for 6% of the time, Pallas kernels for 0%

commit v1 on v0

--- a/solution.py
+++ b/solution.py
@@ -1,3 +1,4 @@
+import functools
 import math
 import jax
 import jax.numpy as jnp
@@ -5,6 +6,29 @@
 from jax.sharding import PartitionSpec as P
 
 very_low = -1e30
+
+
+def post_floor_over_axis(sheet, dim_no):
+    base_arr = list(sheet.shape[1:])
+    base_arr[dim_no] *= sheet.shape[0]
+    p_next = jnp.moveaxis(sheet, 0, dim_no).reshape(base_arr)
+    return p_next
+
+
+def wrap_record(field, row_axis, on_dim):
+    n_all = lax.axis_size(row_axis)
+    bank = tuple(((i0, (i0 + 1) % n_all) for i0 in range(n_all)))
+    queue = [field]
+    while len(queue) < n_all:
+        known = lax.ppermute(queue[-1], row_axis, bank)
+        queue.append(known)
+    z = lax.axis_index(row_axis)
+    queue = jnp.stack(queue, axis=0)[(z - jnp.arange(n_all)) % n_all]
+    side_arr = post_floor_over_axis(queue, on_dim)
+    return side_arr
+
+
+fit_vectors_all = functools.partial(wrap_record, row_axis=("pb", "wa"), on_dim=0)
 
 
 def joined(array, axis, combine):
@@ -226,7 +250,7 @@
     pair_data = jnp.concatenate([queries, out_grads], axis=1)
     look_grid = lookback.reshape(pb_size, ka_size, pair_rows)
     tile_base = pb_index * (ka_size * pair_rows)
-    key_tile = lax.all_gather(key_side, ("pb", "wa"), axis=0, tiled=True)
+    key_tile = fit_vectors_all(key_side)
     row_ids = jnp.arange(key_tile.shape[0], dtype=jnp.int32)
     key_pos = (
         row_ids // pair_rows * (ka_size * pair_rows) + ka_index * pair_rows + row_ids % pair_rows

time: 103 us -> 124 us (1.20)
  waiting for transfers between devices: 9.76 us -> 52.6 us
  blocking collectives: 57.5 us -> 24.8 us
  local copies, waits for them, and re-layouts: 1.25 us -> 9.55 us
  matrix products: 17 us -> 18.3 us
    ppermute x0 -> x7, waiting for transfers between devices: none -> 40.8 us  [wrap_record(): known = lax.ppermute(queue[-1], row_axis, bank)]
    all_gather x1 -> x0, blocking collectives: 32.1 us -> none  [shards(): key_tile = lax.all_gather(key_side, ('pb', 'wa'), axis=0, tiled=True)]
    unnamed x13 -> x25, local copies, waits for them, and re-layouts: 1.24 us -> 5.89 us
    gather x0 -> x2, local copies, waits for them, and re-layouts: none -> 3.01 us  [wrap_record(): queue = jnp.stack(queue, axis=0)[(z - jnp.arange(n_all)) % n_all]]
    reduce_scatter x1, waiting for transfers between devices: 0.01 us -> 2.04 us  [shards(): lax.psum_scatter(query_terms, 'wa', scatter_dimension=1, tiled=True)]
    unnamed x0 -> x1, other arithmetic: none -> 1.58 us
  transfers between devices with their start and end apart: 2 -> 9, of which waited for: 1 -> 9; matrix products, arithmetic and copies ran while one was open for 6% -> 10% of each run, Pallas kernels for 0% -> 0%
where the time goes in v1:
time: 124 us
  waiting for transfers between devices  52.6 us (42%)
  blocking collectives  24.8 us (20%)
  matrix products  18.3 us (15%)
  between operations  14.3 us (12%)
  local copies, waits for them, and re-layouts  9.55 us (8%)
  other arithmetic  4 us (3%)
    ppermute x7, waiting for transfers between devices, wrap_record(): known = lax.ppermute(queue[-1], row_axis, bank)  40.8 us
    unnamed x1, blocking collectives  17.1 us
    reduce_scatter x1, waiting for transfers between devices, shards(): lax.psum_scatter(jnp.concatenate([jnp.dot(clean_rows, side_weight, prefer...  9.71 us
    unnamed x25, local copies, waits for them, and re-layouts  5.89 us
    all_gather x3, blocking collectives, joined(): everything = jax.tree.map(lambda part: lax.all_gather(part, axis), array)  5.44 us
    dot_general x1, matrix products, block_changes(): jnp.einsum('bhd,kd->bhk', query_block, noised_block, preferred_element_ty...  4.67 us
    dot_general x1, matrix products, shards(): jnp.dot(clean_rows, query_weight, preferred_element_type=jnp.float32)  4.25 us
    gather x2, local copies, waits for them, and re-layouts, wrap_record(): queue = jnp.stack(queue, axis=0)[(z - jnp.arange(n_all)) % n_all]  3.01 us
  transfers between devices with their start and end apart: 9, of which 9 were waited for; matrix products, arithmetic and copies ran while one was open for 10% of the time, Pallas kernels for 0%

profile of v1, /device:TPU:0, one launch (start us, length us, event | category | flops | bytes accessed | tf_op | source)
XLA Modules:
  0.0 124.1 jit_solution(5941340598718557580)
XLA Ops:
  6.5 0.0 copy-start
  6.5 0.0 reduce-scatter.5.cloned.1.call-start
  6.5 2.8 %fusion.49 = f32[256,128]{0,1:T(8,128)S(1)} fusion(bf16[256,4096]{1,0:T(8,128)(2,1)} %param.8, bf16[4096,128]{1,0:T(8,128)(2,1)} %param.10), kind=kOutput, calls=%fused_computation.93 | convolution fusion | flops 268435456 | bytes 3276800 | tf_op jit(solution)/shard_map/dot_general | solution.py:242
  9.4 0.0 copy-done
  9.4 2.3 %fusion.10 = f32[256,256]{0,1:T(8,128)S(1)} fusion(bf16[256,4096]{1,0:T(8,128)(2,1)S(1)} %copy-done, bf16[4096,128]{1,0:T(8,128)(2,1)} %param.11, bf16[4096,128]{1,0:T(8,128)(2,1)} %param.10), kind=kOutput, calls=%fused_computation.20 | convolution fusion | flops 541065216 | bytes 4456448 | tf_op jit(solution)/shard_map/dot_general | solution.py:241
  11.7 0.8 pad_maximum_fusion
  12.5 0.0 reduce-scatter.5.cloned.1.call-update
  12.5 0.0 copy-start.5
  12.5 0.0 copy-start.6
  12.5 0.0 copy-start.4
  12.5 0.0 reduce-scatter.3.cloned.1.call-start
  12.6 4.3 %fusion.48 = f32[256,512]{1,0:T(8,128)} fusion(bf16[256,4096]{1,0:T(8,128)(2,1)S(1)} %copy-done, bf16[4096,512]{1,0:T(8,128)(2,1)} %param.9), kind=kOutput, calls=%fused_computation.92 | convolution fusion | flops 1073741824 | bytes 6815744 | tf_op jit(solution)/shard_map/dot_general | solution.py:234
  16.8 0.0 reduce-scatter.3.cloned.1.call-update
  16.9 0.0 copy-done.5
  17.0 0.0 copy-done.6
  17.0 0.6 dynamic-slice
  18.2 0.6 fusion.9
  18.8 9.7 %reduce-scatter.5.cloned.1.call-done = f32[128,384]{0,1:T(8,128)} async-done(((f32[256,384]{0,1:T(8,128)}), f32[128,384]{0,1:T(8,128)}) %reduce-scatter.5.cloned.1.call-update) | async-done | bytes 196624 | tf_op jit(solution)/shard_map/reduce_scatter | solution.py:238
  28.5 1.6 %bitcast_dynamic-update-slice_fusion.7 = (bf16[8,128,384]{1,2,0:T(8,128)(2,1)}, bf16[128,384]{0,1:T(8,128)(2,1)S(1)}) fusion(f32[128,384]{0,1:T(8,128)} %reduce-scatter.5.cloned.1.call-done), kind=kLoop, calls=%fused_computation.43 | loop fusion | flops 49151 | bytes 393216
  30.1 0.4 collective-permute-start
  30.5 7.0 %collective-permute-done = bf16[128,384]{0,1:T(8,128)(2,1)S(1)} collective-permute-done((bf16[128,384]{0,1:T(8,128)(2,1)S(1)}, bf16[128,384]{0,1:T(8,128)(2,1)S(1)}, u32[]{:S(2)}, u32[]{:S(2)}) %collective-permute-start) | collective-permute-done | bytes 98336 | tf_op jit(solution)/shard_map/ppermute | solution.py:23
  37.4 0.0 collective-permute-start.1
  37.4 0.6 bitcast_dynamic-update-slice_fusion.6
  38.1 6.8 %collective-permute-done.1 = bf16[128,384]{0,1:T(8,128)(2,1)S(1)} collective-permute-done((bf16[128,384]{0,1:T(8,128)(2,1)S(1)}, bf16[128,384]{0,1:T(8,128)(2,1)S(1)}, u32[]{:S(2)}, u32[]{:S(2)}) %collective-permute-start.1) | collective-permute-done | bytes 98336 | tf_op jit(solution)/shard_map/ppermute | solution.py:23
  44.9 0.0 collective-permute-start.2
  44.9 0.7 bitcast_dynamic-update-slice_fusion.5
  45.5 2.0 %reduce-scatter.3.cloned.1.call-done = f32[256,256]{1,0:T(8,128)} async-done(((f32[256,512]{1,0:T(8,128)}), f32[256,256]{1,0:T(8,128)}) %reduce-scatter.3.cloned.1.call-update) | async-done | bytes 262160 | tf_op jit(solution)/shard_map/reduce_scatter | solution.py:235
  47.6 1.0 convert_element_type.6
  48.5 0.0 copy-done.4
  48.6 2.2 %all_gather.15 = bf16[512,512]{1,0:T(8,128)(2,1)S(1)} all-gather(bf16[256,512]{1,0:T(8,128)(2,1)S(1)} %pad_maximum_fusion.1), channel_id=1, replica_groups=mesh['pairs'=2,'pb'=4,'ka'=2,'wa'=2] {'ka'}, dimensions={0}, use_global_device_ids=true | all-gather | bytes 786432 | tf_op jit(solution)/shard_map/all_gather | solution.py:259
  50.7 0.8 slice_bitcast_fusion.7
  51.6 0.6 collective-permute-done.2
  52.2 0.2 collective-permute-start.3
  52.3 0.6 bitcast_dynamic-update-slice_fusion.4
  53.0 6.5 %collective-permute-done.3 = bf16[128,384]{0,1:T(8,128)(2,1)S(1)} collective-permute-done((bf16[128,384]{0,1:T(8,128)(2,1)S(1)}, bf16[128,384]{0,1:T(8,128)(2,1)S(1)}, u32[]{:S(2)}, u32[]{:S(2)}) %collective-permute-start.3) | collective-permute-done | bytes 98336 | tf_op jit(solution)/shard_map/ppermute | solution.py:23
  59.5 0.0 collective-permute-start.4
  59.5 0.6 bitcast_dynamic-update-slice_fusion.3
  60.1 6.7 %collective-permute-done.4 = bf16[128,384]{0,1:T(8,128)(2,1)S(1)} collective-permute-done((bf16[128,384]{0,1:T(8,128)(2,1)S(1)}, bf16[128,384]{0,1:T(8,128)(2,1)S(1)}, u32[]{:S(2)}, u32[]{:S(2)}) %collective-permute-start.4) | collective-permute-done | bytes 98336 | tf_op jit(solution)/shard_map/ppermute | solution.py:23
  66.8 0.0 collective-permute-start.5
  66.8 0.6 bitcast_dynamic-update-slice_fusion.2
  67.4 6.7 %collective-permute-done.5 = bf16[128,384]{0,1:T(8,128)(2,1)S(1)} collective-permute-done((bf16[128,384]{0,1:T(8,128)(2,1)S(1)}, bf16[128,384]{0,1:T(8,128)(2,1)S(1)}, u32[]{:S(2)}, u32[]{:S(2)}) %collective-permute-start.5) | collective-permute-done | bytes 98336 | tf_op jit(solution)/shard_map/ppermute | solution.py:23
  74.1 0.0 collective-permute-start.6
  74.1 0.6 bitcast_dynamic-update-slice_fusion.1
  74.7 6.7 %collective-permute-done.6 = bf16[128,384]{0,1:T(8,128)(2,1)S(1)} collective-permute-done((bf16[128,384]{0,1:T(8,128)(2,1)S(1)}, bf16[128,384]{0,1:T(8,128)(2,1)S(1)}, u32[]{:S(2)}, u32[]{:S(2)}) %collective-permute-start.6) | collective-permute-done | bytes 98336 | tf_op jit(solution)/shard_map/ppermute | solution.py:23
  81.4 0.6 bitcast_dynamic-update-slice_fusion
  82.1 1.8 %gather_fusion = bf16[8,128,384]{1,2,0:T(8,128)(2,1)S(1)} fusion(bf16[8,128,384]{1,2,0:T(8,128)(2,1)} %bitcast_dynamic-update-slice_fusion, s32[1024]{0:T(1024)S(1)} %pad_clamp_fusion), kind=kCustom, calls=%fused_computation | custom fusion | bytes 1572896 | tf_op jit(solution)/shard_map/gather | solution.py:26
  83.9 1.2 copy.15
  85.1 0.0 copy-start.1
  85.1 0.0 copy-start.3
  85.1 2.2 %select_reduce_fusion.1 = (f32[512,2]{0,1:T(2,128)S(1)}, f32[512,2,1024]{2,0,1:T(8,128)S(1)}) fusion(pred[512,1024]{1,0:T(8,128)(4,1)S(1)} %fusion.9, bf16[1024,384]{1,0:T(8,128)(2,1)} %bitcast.134, bf16[64,2,8,128]{3,2,1,0:T(8,128)(2,1)} %get-tuple-element.112), kind=kOutput, calls=%fused_computation.11 | convolution fusion | flops 271580160 | bytes 5246976 | tf_op jit(solution)/shard_map/while/body/eval_jaxpr/bhd,kd->bhk/dot_general | solution.py:68
  87.3 0.0 copy-done.1
  87.3 0.0 copy-done.3
  87.3 0.0 copy-start.2
  87.3 2.1 %fusion.4 = (f32[512,2]{0,1:T(2,128)S(1)}, f32[512,2]{0,1:T(2,128)S(1)}, f32[512,2,1024]{2,0,1:T(8,128)S(1)}) fusion(f32[512,2,1024]{2,0,1:T(8,128)S(1)} %get-tuple-element.118, f32[512,2]{0,1:T(2,128)S(1)} %get-tuple-element.117, pred[512,1024]{1,0:T(8,128)(4,1)S(1)} %fusion.9, bf16[1024,384]{1,0:T(8,128)(2,1)S(1)} %bitcast.135, ...), kind=kOutput, calls=%fused_computation.14 | convolution fusion | flops 275773440 | bytes 9449472 | tf_op jit(solution)/shard_map/while/body/eval_jaxpr/bhd,kd->bhk/dot_general | solution.py:71
  89.4 1.8 %all_gather.16 = f32[2,512,2]{1,2,0:T(2,128)S(1)} all-gather(f32[1,512,2]{1,2,0:T(2,128)S(1)} %get-tuple-element.114), channel_id=1, replica_groups=mesh['pairs'=2,'pb'=4,'ka'=2,'wa'=2] {'ka'}, dimensions={0}, use_global_device_ids=true | all-gather | bytes 12288 | tf_op jit(solution)/shard_map/all_gather | solution.py:35
  91.2 1.8 %all_gather.17 = f32[2,512,2]{1,2,0:T(2,128)S(1)} all-gather(f32[1,512,2]{1,2,0:T(2,128)S(1)} %get-tuple-element.116), channel_id=1, replica_groups=mesh['pairs'=2,'pb'=4,'ka'=2,'wa'=2] {'ka'}, dimensions={0}, use_global_device_ids=true | all-gather | bytes 12288 | tf_op jit(solution)/shard_map/all_gather | solution.py:35
  93.1 1.8 %all_gather.18 = f32[2,512,2]{1,2,0:T(2,128)S(1)} all-gather(f32[1,512,2]{1,2,0:T(2,128)S(1)} %get-tuple-element.115), channel_id=1, replica_groups=mesh['pairs'=2,'pb'=4,'ka'=2,'wa'=2] {'ka'}, dimensions={0}, use_global_device_ids=true | all-gather | bytes 12288 | tf_op jit(solution)/shard_map/all_gather | solution.py:35
  94.9 0.0 copy-done.2
  94.9 4.7 %select_reduce_fusion = f32[1024]{0:T(1024)S(1)} fusion(f32[512,2,1024]{2,0,1:T(8,128)S(1)} %get-tuple-element.142, f32[512,2,1024]{2,0,1:T(8,128)S(1)} %get-tuple-element.118, f32[512,2]{0,1:T(2,128)S(1)} %get-tuple-element.94, f32[512,2]{0,1:T(2,128)S(1)} %get-tuple-element.107, f32[512,2]{0,1:T(2,128)S(1)} %get-tuple-element.109, ...), kind=kOutput, calls=%fused_computation.8 | convolution fusion | flops 288357376 | bytes 9457664 | tf_op jit(solution)/shard_map/while/body/eval_jaxpr/while/body/eval_jaxpr/bhd,kd->bhk/dot_general | solution.py:99
  99.6 17.1 %all-reduce = f32[1024]{0:T(1024)S(1)} all-reduce(f32[1024]{0:T(1024)S(1)} %select_reduce_fusion), channel_id=4, replica_groups=mesh['pairs'=2,'pb'=4,'ka'=2,'wa'=2] {'pb','wa'}, use_global_device_ids=true, to_apply=%region_6.7.clone | all-reduce | flops 1024 | bytes 8192
  116.7 0.6 dynamic-slice.1
  (10 shorter events, 0.1 us)
Async XLA Ops:
  6.5 2.8 %copy-start = (bf16[256,4096]{1,0:T(8,128)(2,1)S(1)}, bf16[256,4096]{1,0:T(8,128)(2,1)}, u32[]{:S(2)}) copy-start(bf16[256,4096]{1,0:T(8,128)(2,1)} %param.7) | copy-start | bytes 6291460
  6.5 22.0 %reduce-scatter.5.cloned.1.call-start = ((), (), s32[]{:S(2)}) async-start(), calls=%async_computation.3 | async-start | bytes 589824 | tf_op jit(solution)/shard_map/reduce_scatter | solution.py:238
  12.5 4.4 %copy-start.5 = (s32[2048]{0:T(1024)S(1)}, s32[2048]{0:T(1024)}, u32[]{:S(2)}) copy-start(s32[2048]{0:T(1024)} %param.13) | copy-start | bytes 24580
  12.5 4.5 %copy-start.6 = (u32[32]{0:T(128)S(1)}, u32[32]{0:T(128)}, u32[]{:S(2)}) copy-start(u32[32]{0:T(128)} %constant.152) | copy-start | bytes 388
  12.5 36.0 %copy-start.4 = (bf16[256,256]{1,0:T(8,128)(2,1)S(1)}, bf16[256,256]{1,0:T(8,128)(2,1)}, u32[]{:S(2)}) copy-start(bf16[256,256]{1,0:T(8,128)(2,1)} %param.12) | copy-start | bytes 393220
  12.5 35.0 %reduce-scatter.3.cloned.1.call-start = ((), (), s32[]{:S(2)}) async-start(), calls=%async_computation.2 | async-start | bytes 786432 | tf_op jit(solution)/shard_map/reduce_scatter | solution.py:235
  30.1 7.3 %collective-permute-start = (bf16[128,384]{0,1:T(8,128)(2,1)S(1)}, bf16[128,384]{0,1:T(8,128)(2,1)S(1)}, u32[]{:S(2)}, u32[]{:S(2)}) collective-permute-start(bf16[128,384]{0,1:T(8,128)(2,1)S(1)} %get-tuple-element.111), channel_id=1, source_target_pairs={{0,1},{1,4},{4,5},{5,8},{8,9},{9,12},{12,13},{13,0},{2,3},{3,6},{6... | collective-permute-start | bytes 294920 | tf_op jit(solution)/shard_map/ppermute | solution.py:23
  37.4 7.4 %collective-permute-start.1 = (bf16[128,384]{0,1:T(8,128)(2,1)S(1)}, bf16[128,384]{0,1:T(8,128)(2,1)S(1)}, u32[]{:S(2)}, u32[]{:S(2)}) collective-permute-start(bf16[128,384]{0,1:T(8,128)(2,1)S(1)} %collective-permute-done), channel_id=1, source_target_pairs={{0,1},{1,4},{4,5},{5,8},{8,9},{9,12},{12,13},{13,0},{2,3},{3,6},{6... | collective-permute-start | bytes 294920 | tf_op jit(solution)/shard_map/ppermute | solution.py:23
  44.9 7.3 %collective-permute-start.2 = (bf16[128,384]{0,1:T(8,128)(2,1)S(1)}, bf16[128,384]{0,1:T(8,128)(2,1)S(1)}, u32[]{:S(2)}, u32[]{:S(2)}) collective-permute-start(bf16[128,384]{0,1:T(8,128)(2,1)S(1)} %collective-permute-done.1), channel_id=1, source_target_pairs={{0,1},{1,4},{4,5},{5,8},{8,9},{9,12},{12,13},{13,0},{2,3},{3,6},{6... | collective-permute-start | bytes 294920 | tf_op jit(solution)/shard_map/ppermute | solution.py:23
  52.2 7.3 %collective-permute-start.3 = (bf16[128,384]{0,1:T(8,128)(2,1)S(1)}, bf16[128,384]{0,1:T(8,128)(2,1)S(1)}, u32[]{:S(2)}, u32[]{:S(2)}) collective-permute-start(bf16[128,384]{0,1:T(8,128)(2,1)S(1)} %collective-permute-done.2), channel_id=1, source_target_pairs={{0,1},{1,4},{4,5},{5,8},{8,9},{9,12},{12,13},{13,0},{2,3},{3,6},{6... | collective-permute-start | bytes 294920 | tf_op jit(solution)/shard_map/ppermute | solution.py:23
  59.5 7.3 %collective-permute-start.4 = (bf16[128,384]{0,1:T(8,128)(2,1)S(1)}, bf16[128,384]{0,1:T(8,128)(2,1)S(1)}, u32[]{:S(2)}, u32[]{:S(2)}) collective-permute-start(bf16[128,384]{0,1:T(8,128)(2,1)S(1)} %collective-permute-done.3), channel_id=1, source_target_pairs={{0,1},{1,4},{4,5},{5,8},{8,9},{9,12},{12,13},{13,0},{2,3},{3,6},{6... | collective-permute-start | bytes 294920 | tf_op jit(solution)/shard_map/ppermute | solution.py:23
  66.8 7.3 %collective-permute-start.5 = (bf16[128,384]{0,1:T(8,128)(2,1)S(1)}, bf16[128,384]{0,1:T(8,128)(2,1)S(1)}, u32[]{:S(2)}, u32[]{:S(2)}) collective-permute-start(bf16[128,384]{0,1:T(8,128)(2,1)S(1)} %collective-permute-done.4), channel_id=1, source_target_pairs={{0,1},{1,4},{4,5},{5,8},{8,9},{9,12},{12,13},{13,0},{2,3},{3,6},{6... | collective-permute-start | bytes 294920 | tf_op jit(solution)/shard_map/ppermute | solution.py:23
  74.1 7.3 %collective-permute-start.6 = (bf16[128,384]{0,1:T(8,128)(2,1)S(1)}, bf16[128,384]{0,1:T(8,128)(2,1)S(1)}, u32[]{:S(2)}, u32[]{:S(2)}) collective-permute-start(bf16[128,384]{0,1:T(8,128)(2,1)S(1)} %collective-permute-done.5), channel_id=1, source_target_pairs={{0,1},{1,4},{4,5},{5,8},{8,9},{9,12},{12,13},{13,0},{2,3},{3,6},{6... | collective-permute-start | bytes 294920 | tf_op jit(solution)/shard_map/ppermute | solution.py:23
  85.1 2.2 %copy-start.1 = (bf16[8,128,384]{2,1,0:T(8,128)(2,1)S(1)}, bf16[8,128,384]{2,1,0:T(8,128)(2,1)}, u32[]{:S(2)}) copy-start(bf16[8,128,384]{2,1,0:T(8,128)(2,1)} %copy.15) | copy-start | bytes 2359300
  85.1 2.2 %copy-start.3 = (bf16[64,2,8,128]{3,2,1,0:T(8,128)(2,1)S(1)}, bf16[64,2,8,128]{3,2,1,0:T(8,128)(2,1)}, u32[]{:S(2)}) copy-start(bf16[64,2,8,128]{3,2,1,0:T(8,128)(2,1)} %get-tuple-element.113) | copy-start | bytes 786436
  87.3 7.6 %copy-start.2 = (bf16[64,2,8,128]{3,2,1,0:T(8,128)(2,1)S(1)}, bf16[64,2,8,128]{3,2,1,0:T(8,128)(2,1)}, u32[]{:S(2)}) copy-start(bf16[64,2,8,128]{3,2,1,0:T(8,128)(2,1)} %get-tuple-element.112) | copy-start | bytes 786436
Sparse Core Ops, SparseCore 0:
  12.6 15.8 reduce-scatter.4
  30.8 16.7 reduce-scatter.2
